TPU v7x, 256 devices: a whole 4x4x8 slice. The times are simulated.
256 devices in a mesh: section: 2 (over y_hi), seq: 32 (over x, z), chan: 4 (over y_lo, core).
Axes of the slice: x: 4, y: 4 (y_hi: 2, y_lo: 2; y = y_hi * 2 + y_lo), z: 8, core: 2. Of those that a mesh axis runs over, the one named last changes fastest.
Arguments:
- bases: int32 [2, 2097152], P('section', 'seq'), may hold values from 0 to 3
- stem_embedding_weight: bfloat16 [512, 1536], P(None, 'chan'), may hold values from -1.64443437 to 1.64443437
- gains: float32 [3, 1536], replicated, may hold values from 0.1 to 1.9
- conv_weight: bfloat16 [3, 3, 1536, 1536], P(None, None, None, 'chan'), may hold values from -0.09375 to 0.09375
- dec_weight: bfloat16 [1536, 384], P('chan'), may hold values from -0.3125 to 0.3125
- upstream: bfloat16 [2, 16384, 1536], P('section', 'seq', 'chan'), may hold values from -0.032958984 to 0.032958984
Outputs:
- decoded: bfloat16 [2, 16384, 1536], P('section', 'seq', 'chan')
- weight_grad: float32 [1536, 384], P('chan')
All inputs are finite; a program needn't handle non-finite values.
Results may differ from a plain program's by a relative error of at most 0.0076.
Values may be sent and summed in bfloat16 or wider, within the bound.
No kernel may reach another device: no remote copies, remote signals or barrier semaphores. Data moves between devices by JAX's collectives and lax.ppermute only.
A program may use at most 128 MiB of HBM per device.

v0:
```python
import jax
import jax.numpy as jnp
from jax import lax
from jax.sharding import PartitionSpec as P

PATCH = 128
FIRST_DILATION0 = 2
EPSILON = 1e-06


def with_halo(shard, sides, width):
    for axis, dim in sides:
        size, length = (lax.axis_size(axis), shard.shape[dim])
        up = [(i, (i + 1) % size) for i in range(size - 1)]
        down = [(j, i) for i, j in up]
        last = lax.slice_in_dim(shard, length - width, length, axis=dim)
        initial = lax.slice_in_dim(shard, 0, width, axis=dim)
        before = lax.ppermute(last, axis, up)
        after = lax.ppermute(initial, axis, down)
        shard = jnp.concatenate([before, shard, after], axis=dim)
    return shard


def activate(rows, gain_row):
    widened = rows.astype(jnp.float32)
    inverse_rms = lax.rsqrt(jnp.mean(widened * widened, axis=-1, keepdims=True) + EPSILON)
    return jax.nn.gelu(widened * inverse_rms * gain_row).astype(jnp.bfloat16)


def apply_convolution(padded, kernel_taps, dilation_step, row_count):
    update = jnp.dot(padded[0:row_count], kernel_taps[0], preferred_element_type=jnp.float32)
    for offset in range(1, kernel_taps.shape[0]):
        start = offset * dilation_step
        update = update + jnp.dot(
            padded[start : start + row_count],
            kernel_taps[offset],
            preferred_element_type=jnp.float32,
        )
    return update


def body(bases, stem_embedding_weight, gains, conv_weight, dec_weight, upstream):
    row_count = upstream.shape[1]
    letters = bases.reshape(row_count, PATCH)
    onehot = letters[:, :, None] == jnp.arange(4, dtype=jnp.int32)[None, None, :]
    onehot = onehot.astype(jnp.bfloat16).reshape(row_count, PATCH * 4)
    stream = jnp.dot(onehot, stem_embedding_weight, preferred_element_type=jnp.float32).astype(
        jnp.bfloat16
    )
    for tower_layer_index in range(conv_weight.shape[0]):
        dilation_step = FIRST_DILATION0 * 2**tower_layer_index
        full_rows = lax.all_gather(stream, "chan", axis=1, tiled=True)
        padded = with_halo(
            activate(full_rows, gains[tower_layer_index]), (("seq", 0),), dilation_step
        )
        update = apply_convolution(padded, conv_weight[tower_layer_index], dilation_step, row_count)
        stream = (stream.astype(jnp.float32) + update).astype(jnp.bfloat16)
    decoded = jnp.dot(stream, dec_weight, preferred_element_type=jnp.float32).astype(jnp.bfloat16)
    upstream_rows = upstream[0]
    contract_row_pairs = (((0,), (0,)), ((), ()))
    partial_grad = lax.dot_general(
        stream, upstream_rows, contract_row_pairs, preferred_element_type=jnp.float32
    )
    weight_grad = lax.psum(partial_grad, ("section", "seq"))
    return (decoded[None], weight_grad)


def solution(mesh):
    placed = (
        P("section", "seq"),
        P(None, "chan"),
        P(),
        P(None, None, None, "chan"),
        P("chan", None),
        P("section", "seq", "chan"),
    )
    return jax.shard_map(
        body,
        mesh=mesh,
        in_specs=placed,
        out_specs=(P("section", "seq", "chan"), P("chan", None)),
        check_vma=False,
    )
```

profile of v0, /device:TPU:24, one launch (start us, length us, event | category | flops | bytes accessed | tf_op | source)
XLA Modules:
  0.0 813.8 jit_solution(4729358638135030658)
XLA Ops:
  7.2 0.0 copy-start
  7.2 0.0 all-gather.4.cloned.1.call-start
  7.2 0.1 eq.26
  7.4 1.1 copy.8
  8.4 0.2 eq.23
  8.6 0.4 eq.24
  9.0 1.3 convolution_convert_fusion.1
  10.3 0.0 all-gather.4.cloned.1.call-update
  10.4 0.0 all-gather.6.cloned.1.call-start
  10.4 0.1 slice_reduce_fusion
  10.5 29.4 %all-gather.4.cloned.1.call-done = bf16[512,1536]{1,0:T(8,128)(2,1)} async-done(((bf16[512,384]{1,0:T(8,128)(2,1)}), bf16[512,1536]{1,0:T(8,128)(2,1)}) %all-gather.4.cloned.1.call-update) | async-done | bytes 1572880 | tf_op jit(solution)/shard_map/all_gather | solution.py:52
  39.8 1.8 fusion
  41.6 2.8 fusion.4
  44.5 3.5 collective-permute-start
  47.9 1.3 collective-permute-start.1
  49.2 2.2 fusion.60
  51.5 0.0 copy-start.1
  51.5 2.0 collective-permute-done.1
  53.4 2.3 fusion.38
  55.7 3.1 fusion.49
  58.8 0.0 all-gather.6.cloned.1.call-update
  58.8 0.0 all-gather.8.cloned.1.call-start
  58.8 28.8 %all-gather.6.cloned.1.call-done = bf16[512,1536]{1,0:T(8,128)(2,1)} async-done(((bf16[512,384]{1,0:T(8,128)(2,1)}), bf16[512,1536]{1,0:T(8,128)(2,1)}) %all-gather.6.cloned.1.call-update) | async-done | bytes 1572880 | tf_op jit(solution)/shard_map/all_gather | solution.py:52
  87.6 1.8 fusion.9
  89.4 2.8 fusion.13
  92.2 1.3 collective-permute-start.3
  93.5 2.2 fusion.56
  95.8 0.0 copy-start.3
  95.8 4.7 collective-permute-start.2
  100.5 2.3 fusion.34
  102.8 3.0 add_convert_fusion.1
  105.8 0.0 all-gather.8.cloned.1.call-update
  105.9 0.0 all-reduce.2.cloned.1.call-start
  105.9 29.4 %all-gather.8.cloned.1.call-done = bf16[512,1536]{1,0:T(8,128)(2,1)} async-done(((bf16[512,384]{1,0:T(8,128)(2,1)}), bf16[512,1536]{1,0:T(8,128)(2,1)}) %all-gather.8.cloned.1.call-update) | async-done | bytes 1572880 | tf_op jit(solution)/shard_map/all_gather | solution.py:52
  135.3 1.8 fusion.18
  137.1 2.8 fusion.22
  139.9 1.5 collective-permute-start.5
  141.4 2.2 fusion.52
  143.7 0.0 copy-start.2
  143.7 4.7 collective-permute-start.4
  148.4 2.2 fusion.30
  150.6 0.0 copy-start.5
  150.7 2.3 add_convert_fusion
  153.0 1.2 fusion.74
  154.3 0.0 all-reduce.2.cloned.1.call-update
  154.3 1.1 fusion.50
  155.4 649.9 %all-reduce.2.cloned.1.call-done = f32[384,384]{1,0:T(8,128)} async-done(((f32[384,384]{1,0:T(8,128)}), f32[384,384]{1,0:T(8,128)}) %all-reduce.2.cloned.1.call-update) | async-done | bytes 589840 | tf_op jit(solution)/shard_map/psum | solution.py:64
  805.3 1.9 copy.10
  (21 shorter events, 0.1 us)
Async XLA Ops:
  7.2 1.8 copy-start
  7.2 3.2 copy-start.6
  7.2 32.7 %all-gather.4.cloned.1.call-start = ((), (), s32[]{:S(2)}) async-start(), calls=%async_computation | async-start | bytes 1966080 | tf_op jit(solution)/shard_map/all_gather | solution.py:52
  10.4 77.3 %all-gather.6.cloned.1.call-start = ((), (), s32[]{:S(2)}) async-start(), calls=%async_computation.1 | async-start | bytes 1966080 | tf_op jit(solution)/shard_map/all_gather | solution.py:52
  44.5 11.2 %collective-permute-start = (bf16[2,1536]{1,0:T(2,128)(2,1)S(1)}, bf16[2,1536]{1,0:T(2,128)(2,1)S(1)}, u32[]{:S(2)}, u32[]{:S(2)}) collective-permute-start(bf16[2,1536]{1,0:T(2,128)(2,1)S(1)} %get-tuple-element.9), channel_id=1, source_target_pairs={{0,4},{4,8},{8,12},{12,16},{16,20},{20,24},{24,28},{28,32},{32,36}... | collective-permute-start | bytes 18440 | tf_op jit(solution)/shard_map/ppermute | solution.py:18
  47.9 5.5 collective-permute-start.1
  51.5 4.2 copy-start.1
  58.8 76.5 %all-gather.8.cloned.1.call-start = ((), (), s32[]{:S(2)}) async-start(), calls=%async_computation.2 | async-start | bytes 1966080 | tf_op jit(solution)/shard_map/all_gather | solution.py:52
  92.2 8.3 %collective-permute-start.3 = (bf16[4,1536]{1,0:T(4,128)(2,1)S(1)}, bf16[4,1536]{1,0:T(4,128)(2,1)S(1)}, u32[]{:S(2)}, u32[]{:S(2)}) collective-permute-start(bf16[4,1536]{1,0:T(4,128)(2,1)S(1)} %get-tuple-element.8), channel_id=1, source_target_pairs={{4,0},{8,4},{12,8},{16,12},{20,16},{24,20},{28,24},{32,28},{36,32}... | collective-permute-start | bytes 36872 | tf_op jit(solution)/shard_map/ppermute | solution.py:19
  95.8 7.0 copy-start.3
  95.8 7.0 collective-permute-start.2
  105.9 699.5 %all-reduce.2.cloned.1.call-start = ((), (), s32[]{:S(2)}) async-start(), calls=%async_computation.3 | async-start | bytes 1179648 | tf_op jit(solution)/shard_map/psum | solution.py:64
  139.9 8.4 %collective-permute-start.5 = (bf16[8,1536]{1,0:T(8,128)(2,1)S(1)}, bf16[8,1536]{1,0:T(8,128)(2,1)S(1)}, u32[]{:S(2)}, u32[]{:S(2)}) collective-permute-start(bf16[8,1536]{1,0:T(8,128)(2,1)S(1)} %get-tuple-element.6), channel_id=1, source_target_pairs={{4,0},{8,4},{12,8},{16,12},{20,16},{24,20},{28,24},{32,28},{36,32}... | collective-permute-start | bytes 73736 | tf_op jit(solution)/shard_map/ppermute | solution.py:19
  143.7 7.0 copy-start.2
  143.7 7.0 collective-permute-start.4
  150.6 2.4 copy-start.4
  150.6 3.6 copy-start.5
Sparse Core Ops, SparseCore 0:
  10.5 29.3 all-gather.3
  58.9 28.6 all-gather.5
  106.0 29.3 all-gather.7
  154.4 650.8 all-reduce.1
where the time goes:
time: 815 us; the launch traced here: 814 us
  waiting for transfers between devices  740 us (91%)
  matrix products  25.6 us (3%)
  starting transfers between devices  17 us (2%)
  between operations  14.1 us (2%)
  other arithmetic  13.7 us (2%)
    psum x1, waiting for transfers between devices, body(): weight_grad = lax.psum(partial_grad, ('section', 'seq'))  650 us
    all_gather x3, waiting for transfers between devices, body(): full_rows = lax.all_gather(stream, 'chan', axis=1, tiled=True)  87.6 us
  transfers between devices with their start and end apart: 10, of which 5 were waited for; matrix products, arithmetic and copies ran while one was open for 2% of the time, Pallas kernels for 0%

commit v1 on v0

--- a/solution.py
+++ b/solution.py
@@ -61,7 +61,9 @@
     partial_grad = lax.dot_general(
         stream, upstream_rows, contract_row_pairs, preferred_element_type=jnp.float32
     )
-    weight_grad = lax.psum(partial_grad, ("section", "seq"))
+    weight_grad = partial_grad
+    for rr in ("seq", "section"):
+        weight_grad = lax.psum(weight_grad, axis_name=rr)
     return (decoded[None], weight_grad)
 
 

time: 815 us -> 358 us (0.44)
  waiting for transfers between devices: 740 us -> 281 us
    psum x1 -> x2, waiting for transfers between devices: 650 us -> 191 us  [body(): weight_grad = lax.psum(weight_grad, axis_name=rr)]
  transfers between devices with their start and end apart: 10 -> 11, of which waited for: 5 -> 6; matrix products, arithmetic and copies ran while one was open for 2% -> 4% of each run, Pallas kernels for 0% -> 0%
where the time goes in v1:
time: 358 us; the launch traced here: 355 us
  waiting for transfers between devices  281 us (78%)
  matrix products  25.6 us (7%)
  starting transfers between devices  17.1 us (5%)
  between operations  14.1 us (4%)
  other arithmetic  13.7 us (4%)
  local copies, waits for them, and re-layouts  3.78 us (1%)
    psum x2, waiting for transfers between devices, body(): weight_grad = lax.psum(weight_grad, axis_name=rr)  191 us
    all_gather x3, waiting for transfers between devices, body(): full_rows = lax.all_gather(stream, 'chan', axis=1, tiled=True)  87.6 us
    dot_general x6, matrix products, apply_convolution(): jnp.dot(padded[start:start + row_count], kernel_taps[offset], preferred_e...  13.5 us
    ppermute x3, starting transfers between devices, with_halo(): before = lax.ppermute(last, axis, up)  12.8 us
    dot_general x3, matrix products, apply_convolution(): jnp.dot(padded[0:row_count], kernel_taps[0], preferred_element_type=jnp.f...  8.45 us
    convert_element_type x3, other arithmetic, activate(): return jax.nn.gelu(widened * inverse_rms * gain_row).astype(jnp.bfloat16)  8.35 us
  transfers between devices with their start and end apart: 11, of which 6 were waited for; matrix products, arithmetic and copies ran while one was open for 4% of the time, Pallas kernels for 0%

profile of v1, /device:TPU:24, one launch (start us, length us, event | category | flops | bytes accessed | tf_op | source)
XLA Modules:
  0.0 354.9 jit_solution(6602686329960665526)
XLA Ops:
  7.2 0.0 copy-start
  7.2 0.0 all-gather.4.cloned.1.call-start
  7.2 0.1 eq.26
  7.4 1.1 copy.8
  8.4 0.2 eq.23
  8.6 0.4 eq.24
  9.0 1.3 convolution_convert_fusion.1
  10.3 0.0 all-gather.4.cloned.1.call-update
  10.4 0.0 all-gather.6.cloned.1.call-start
  10.4 0.1 slice_reduce_fusion
  10.5 29.4 %all-gather.4.cloned.1.call-done = bf16[512,1536]{1,0:T(8,128)(2,1)} async-done(((bf16[512,384]{1,0:T(8,128)(2,1)}), bf16[512,1536]{1,0:T(8,128)(2,1)}) %all-gather.4.cloned.1.call-update) | async-done | bytes 1572880 | tf_op jit(solution)/shard_map/all_gather | solution.py:52
  39.8 1.8 fusion
  41.6 2.8 fusion.4
  44.5 3.5 collective-permute-start
  47.9 1.3 collective-permute-start.1
  49.2 2.2 fusion.60
  51.5 2.0 collective-permute-done.1
  53.4 2.3 fusion.38
  55.7 3.1 fusion.49
  58.8 0.0 all-gather.6.cloned.1.call-update
  58.8 0.0 all-gather.8.cloned.1.call-start
  58.8 28.8 %all-gather.6.cloned.1.call-done = bf16[512,1536]{1,0:T(8,128)(2,1)} async-done(((bf16[512,384]{1,0:T(8,128)(2,1)}), bf16[512,1536]{1,0:T(8,128)(2,1)}) %all-gather.6.cloned.1.call-update) | async-done | bytes 1572880 | tf_op jit(solution)/shard_map/all_gather | solution.py:52
  87.6 1.8 fusion.9
  89.4 2.8 fusion.13
  92.2 1.3 collective-permute-start.3
  93.5 2.2 fusion.56
  95.8 4.7 %collective-permute-start.2 = (bf16[4,1536]{1,0:T(4,128)(2,1)S(1)}, bf16[4,1536]{1,0:T(4,128)(2,1)S(1)}, u32[]{:S(2)}, u32[]{:S(2)}) collective-permute-start(bf16[4,1536]{1,0:T(4,128)(2,1)S(1)} %get-tuple-element.7), channel_id=1, source_target_pairs={{0,4},{4,8},{8,12},{12,16},{16,20},{20,24},{24,28},{28,32},{32,36}... | collective-permute-start | bytes 36872 | tf_op jit(solution)/shard_map/ppermute | solution.py:18
  100.5 2.3 fusion.34
  102.8 3.0 add_convert_fusion.1
  105.8 0.0 all-gather.8.cloned.1.call-update
  105.9 0.0 all-reduce.3.cloned.1.call-start
  105.9 29.4 %all-gather.8.cloned.1.call-done = bf16[512,1536]{1,0:T(8,128)(2,1)} async-done(((bf16[512,384]{1,0:T(8,128)(2,1)}), bf16[512,1536]{1,0:T(8,128)(2,1)}) %all-gather.8.cloned.1.call-update) | async-done | bytes 1572880 | tf_op jit(solution)/shard_map/all_gather | solution.py:52
  135.3 1.8 fusion.18
  137.1 2.8 fusion.22
  139.9 1.5 collective-permute-start.5
  141.4 2.2 fusion.52
  143.7 0.0 copy-start.2
  143.7 4.7 %collective-permute-start.4 = (bf16[8,1536]{1,0:T(8,128)(2,1)S(1)}, bf16[8,1536]{1,0:T(8,128)(2,1)S(1)}, u32[]{:S(2)}, u32[]{:S(2)}) collective-permute-start(bf16[8,1536]{1,0:T(8,128)(2,1)S(1)} %get-tuple-element.5), channel_id=1, source_target_pairs={{0,4},{4,8},{8,12},{12,16},{16,20},{20,24},{24,28},{28,32},{32,36}... | collective-permute-start | bytes 73736 | tf_op jit(solution)/shard_map/ppermute | solution.py:18
  148.4 2.2 fusion.30
  150.7 2.3 add_convert_fusion
  153.0 1.2 fusion.74
  154.3 0.0 all-reduce.3.cloned.1.call-update
  154.3 0.0 all-reduce.5.cloned.1.call-start
  154.3 150.3 %all-reduce.3.cloned.1.call-done = f32[384,384]{1,0:T(8,128)} async-done(((f32[384,384]{1,0:T(8,128)}), f32[384,384]{1,0:T(8,128)}) %all-reduce.3.cloned.1.call-update) | async-done | bytes 589840 | tf_op jit(solution)/shard_map/psum | solution.py:66
  304.7 0.0 all-reduce.5.cloned.1.call-update
  304.7 1.1 fusion.50
  305.8 40.6 %all-reduce.5.cloned.1.call-done = f32[384,384]{1,0:T(8,128)} async-done(((f32[384,384]{1,0:T(8,128)}), f32[384,384]{1,0:T(8,128)}) %all-reduce.5.cloned.1.call-update) | async-done | bytes 589840 | tf_op jit(solution)/shard_map/psum | solution.py:66
  346.4 1.9 copy.11
  (24 shorter events, 0.1 us)
Async XLA Ops:
  7.2 1.8 copy-start
  7.2 3.2 copy-start.6
  7.2 32.7 %all-gather.4.cloned.1.call-start = ((), (), s32[]{:S(2)}) async-start(), calls=%async_computation | async-start | bytes 1966080 | tf_op jit(solution)/shard_map/all_gather | solution.py:52
  10.4 77.3 %all-gather.6.cloned.1.call-start = ((), (), s32[]{:S(2)}) async-start(), calls=%async_computation.1 | async-start | bytes 1966080 | tf_op jit(solution)/shard_map/all_gather | solution.py:52
  44.5 11.2 %collective-permute-start = (bf16[2,1536]{1,0:T(2,128)(2,1)S(1)}, bf16[2,1536]{1,0:T(2,128)(2,1)S(1)}, u32[]{:S(2)}, u32[]{:S(2)}) collective-permute-start(bf16[2,1536]{1,0:T(2,128)(2,1)S(1)} %get-tuple-element.9), channel_id=1, source_target_pairs={{0,4},{4,8},{8,12},{12,16},{16,20},{20,24},{24,28},{28,32},{32,36}... | collective-permute-start | bytes 18440 | tf_op jit(solution)/shard_map/ppermute | solution.py:18
  47.9 5.5 %collective-permute-start.1 = (bf16[2,1536]{1,0:T(2,128)(2,1)S(1)}, bf16[2,1536]{1,0:T(2,128)(2,1)S(1)}, u32[]{:S(2)}, u32[]{:S(2)}) collective-permute-start(bf16[2,1536]{1,0:T(2,128)(2,1)S(1)} %get-tuple-element.10), channel_id=1, source_target_pairs={{4,0},{8,4},{12,8},{16,12},{20,16},{24,20},{28,24},{32,28},{36,32}... | collective-permute-start | bytes 18440 | tf_op jit(solution)/shard_map/ppermute | solution.py:19
  51.5 4.2 %copy-start.1 = (bf16[512,384]{1,0:T(8,128)(2,1)S(1)}, bf16[512,384]{1,0:T(8,128)(2,1)}, u32[]{:S(2)}) copy-start(bf16[512,384]{1,0:T(8,128)(2,1)} %convolution_convert_fusion.1) | copy-start | bytes 1179652
  58.8 76.5 %all-gather.8.cloned.1.call-start = ((), (), s32[]{:S(2)}) async-start(), calls=%async_computation.2 | async-start | bytes 1966080 | tf_op jit(solution)/shard_map/all_gather | solution.py:52
  92.2 8.3 %collective-permute-start.3 = (bf16[4,1536]{1,0:T(4,128)(2,1)S(1)}, bf16[4,1536]{1,0:T(4,128)(2,1)S(1)}, u32[]{:S(2)}, u32[]{:S(2)}) collective-permute-start(bf16[4,1536]{1,0:T(4,128)(2,1)S(1)} %get-tuple-element.8), channel_id=1, source_target_pairs={{4,0},{8,4},{12,8},{16,12},{20,16},{24,20},{28,24},{32,28},{36,32}... | collective-permute-start | bytes 36872 | tf_op jit(solution)/shard_map/ppermute | solution.py:19
  95.8 7.0 %copy-start.3 = (bf16[512,384]{1,0:T(8,128)(2,1)S(1)}, bf16[512,384]{1,0:T(8,128)(2,1)}, u32[]{:S(2)}) copy-start(bf16[512,384]{1,0:T(8,128)(2,1)} %fusion.49) | copy-start | bytes 1179652
  95.8 7.0 %collective-permute-start.2 = (bf16[4,1536]{1,0:T(4,128)(2,1)S(1)}, bf16[4,1536]{1,0:T(4,128)(2,1)S(1)}, u32[]{:S(2)}, u32[]{:S(2)}) collective-permute-start(bf16[4,1536]{1,0:T(4,128)(2,1)S(1)} %get-tuple-element.7), channel_id=1, source_target_pairs={{0,4},{4,8},{8,12},{12,16},{16,20},{20,24},{24,28},{28,32},{32,36}... | collective-permute-start | bytes 36872 | tf_op jit(solution)/shard_map/ppermute | solution.py:18
  105.9 198.8 %all-reduce.3.cloned.1.call-start = ((), (), s32[]{:S(2)}) async-start(), calls=%async_computation.3 | async-start | bytes 1179648 | tf_op jit(solution)/shard_map/psum | solution.py:66
  139.9 8.4 %collective-permute-start.5 = (bf16[8,1536]{1,0:T(8,128)(2,1)S(1)}, bf16[8,1536]{1,0:T(8,128)(2,1)S(1)}, u32[]{:S(2)}, u32[]{:S(2)}) collective-permute-start(bf16[8,1536]{1,0:T(8,128)(2,1)S(1)} %get-tuple-element.6), channel_id=1, source_target_pairs={{4,0},{8,4},{12,8},{16,12},{20,16},{24,20},{28,24},{32,28},{36,32}... | collective-permute-start | bytes 73736 | tf_op jit(solution)/shard_map/ppermute | solution.py:19
  143.7 7.0 %copy-start.2 = (bf16[512,384]{1,0:T(8,128)(2,1)S(1)}, bf16[512,384]{1,0:T(8,128)(2,1)}, u32[]{:S(2)}) copy-start(bf16[512,384]{1,0:T(8,128)(2,1)} %add_convert_fusion.1) | copy-start | bytes 1179652
  143.7 7.0 %collective-permute-start.4 = (bf16[8,1536]{1,0:T(8,128)(2,1)S(1)}, bf16[8,1536]{1,0:T(8,128)(2,1)S(1)}, u32[]{:S(2)}, u32[]{:S(2)}) collective-permute-start(bf16[8,1536]{1,0:T(8,128)(2,1)S(1)} %get-tuple-element.5), channel_id=1, source_target_pairs={{0,4},{4,8},{8,12},{12,16},{16,20},{20,24},{24,28},{28,32},{32,36}... | collective-permute-start | bytes 73736 | tf_op jit(solution)/shard_map/ppermute | solution.py:18
  150.6 2.4 copy-start.4
  150.6 154.0 %copy-start.5 = (bf16[384,384]{1,0:T(8,128)(2,1)S(1)}, bf16[384,384]{1,0:T(8,128)(2,1)}, u32[]{:S(2)}) copy-start(bf16[384,384]{1,0:T(8,128)(2,1)} %param.10) | copy-start | bytes 884740
  154.3 192.1 %all-reduce.5.cloned.1.call-start = ((), (), s32[]{:S(2)}) async-start(), calls=%async_computation.4 | async-start | bytes 1179648 | tf_op jit(solution)/shard_map/psum | solution.py:66
Sparse Core Ops, SparseCore 0:
  10.5 29.3 all-gather.3
  58.9 28.6 all-gather.5
  106.0 29.3 all-gather.7
  154.4 150.2 all-reduce.2
  307.3 39.0 all-reduce.4
